TPU v7x, 32 devices: a whole 2x2x4 slice. The times are simulated.
32 devices in a mesh: bond: 8 (over z, x), mpo: 4 (over y, core).
Axes of the slice: x: 2, y: 2, z: 4, core: 2. Of those that a mesh axis runs over, the one named last changes fastest.
Arguments:
- wave_blocks: bfloat16 [8, 16, 256, 256], P('bond'), may hold values from -6 to 6
- left_environment: bfloat16 [8, 8, 256, 256], P('mpo', 'bond'), may hold values from -0.375 to 0.375
- right_environment: bfloat16 [8, 8, 256, 256], P('mpo', 'bond'), may hold values from -0.375 to 0.375
- site_operators: bfloat16 [8, 16, 16], P('mpo'), may hold values from -1.1953125 to 1.1953125
- right_sector: int32 [8, 16, 1], P('bond'), may hold values from 0 to 7; in each aligned block of 16 rows (0 to 15, 16 to 31, ..., all dimensions but the last counted through in order) at most 2 rows name the same one
- left_sizes: int32 [8], replicated, may hold values from 128 to 256
- right_sizes: int32 [8], replicated, may hold values from 128 to 256
- sector_place: int32 [8], replicated, may hold values from 0 to 7, each once
Outputs:
- applied: bfloat16 [8, 16, 256, 256], P('bond', 'mpo')
Inputs may be any that keep to these rules, and one draw needn't show every extreme that they name: `right_sector`: among the 16 blocks of one bond index no right sector is named more than 2 times, a bound that some block reaches. `sector_place`: every position is taken by exactly one right sector.
All inputs are finite; a program needn't handle non-finite values.
Results may differ from a plain program's by a relative error of at most 0.0057.
Values may be sent and summed in bfloat16 or wider, within the bound.
A program may use at most 64 MiB of HBM per device.

v0:
```python
import jax
import jax.numpy as jnp
from jax import lax
from jax.sharding import PartitionSpec as P


def lookup(entries, indices):
    count = entries.shape[0]
    matches = indices[..., None] == jnp.arange(count, dtype=jnp.int32)
    return jnp.sum(jnp.where(matches, entries, 0), axis=-1)


def shards(
    wave_blocks,
    left_environment,
    right_environment,
    site_operators,
    right_sector,
    left_sizes,
    right_sizes,
    sector_place,
):
    sectors = wave_blocks.shape[0]
    states = wave_blocks.shape[1]
    block_rows = wave_blocks.shape[2]
    channels = left_environment.shape[0]
    first_sector = lax.axis_index("bond") * sectors
    sector_ids = right_sector[:, :, 0]
    offsets = jnp.arange(block_rows, dtype=jnp.int32)
    left_live = lax.dynamic_slice_in_dim(left_sizes, first_sector, sectors)
    row_mask = offsets[None, :] < left_live[:, None]
    column_mask = offsets[None, None, :] < lookup(right_sizes, sector_ids)[:, :, None]
    live_mask = row_mask[:, None, :, None] & column_mask[:, :, None, :]
    masked = jnp.where(live_mask, wave_blocks, jnp.zeros((), jnp.bfloat16))
    block_count = sectors * states
    flat_blocks = masked.reshape(block_count, block_rows, block_rows)
    place_flat = lookup(sector_place, sector_ids).reshape(block_count)
    gathered = lax.all_gather(right_environment, "bond", axis=1, tiled=True)
    chosen = jnp.take(gathered, place_flat, axis=1)
    right_part = jnp.einsum(
        "bac,hbxc->bhax", flat_blocks, chosen, preferred_element_type=jnp.float32
    ).astype(jnp.bfloat16)
    right_part = right_part.reshape(sectors, states, channels, block_rows, block_rows)
    same_sector = sector_ids[:, :, None] == sector_ids[:, None, :]
    mixing = jnp.where(same_sector[:, None], site_operators[None], jnp.zeros((), jnp.bfloat16))
    mixed = jnp.einsum(
        "nhst,nthac->nshac", mixing, right_part, preferred_element_type=jnp.float32
    ).astype(jnp.bfloat16)
    partial_value = jnp.einsum(
        "hnab,nshbc->nsac", left_environment, mixed, preferred_element_type=jnp.float32
    )
    per_device = states // lax.axis_size("mpo")
    first_state = lax.axis_index("mpo") * per_device
    summed = lax.psum(partial_value, "mpo")
    summed = lax.dynamic_slice_in_dim(summed, first_state, per_device, 1)
    kept_mask = lax.dynamic_slice_in_dim(live_mask, first_state, per_device, 1)
    return jnp.where(kept_mask, summed, jnp.zeros((), jnp.float32)).astype(jnp.bfloat16)


def solution(mesh):
    placed = (
        P("bond", None, None, None),
        P("mpo", "bond", None, None),
        P("mpo", "bond", None, None),
        P("mpo", None, None),
        P("bond", None, None),
        P(),
        P(),
        P(),
    )
    return jax.shard_map(
        shards, mesh=mesh, in_specs=placed, out_specs=P("bond", "mpo", None, None), check_vma=False
    )
```

profile of v0, /device:TPU:0, one launch (start us, length us, event | category | flops | bytes accessed | tf_op | source)
XLA Modules:
  0.0 172.7 jit_solution(5104987714782508854)
XLA Ops:
  6.5 0.0 copy-start
  6.5 0.0 all-gather.2.cloned.1.call-start
  6.6 0.7 all-gather.2.cloned.1.call-update
  7.3 2.9 %copy.12 = bf16[1,16,256,256]{2,3,1,0:T(8,128)(2,1)S(1)} copy(bf16[1,16,256,256]{3,2,1,0:T(8,128)(2,1)} %param.8) | data formatting | bytes 4194304 | tf_op args[0]
  10.2 0.0 copy-done.5
  10.2 0.6 dynamic_slice.9
  10.8 0.6 iota_compare_fusion.2
  11.4 0.0 copy-done.2
  11.4 0.0 copy-done.3
  11.4 0.0 copy-done.4
  11.4 0.1 select_reduce_fusion.1
  11.6 0.1 broadcast_compare_fusion
  11.6 0.1 iota_compare_fusion
  11.7 2.0 %broadcast_and_fusion = pred[1,16,256,256]{2,3,1,0:T(8,128)(4,1)} fusion(pred[16,256]{1,0:T(8,128)(4,1)S(1)} %iota_compare_fusion, pred[256]{0:T(512)(128)(4,1)S(1)} %iota_compare_fusion.2), kind=kLoop, calls=%fused_computation.15 | loop fusion | flops 1048576 | bytes 1052928 | tf_op jit(solution)/shard_map/and | solution.py:33
  13.7 47.6 %all-gather.2.cloned.1.call-done = bf16[2,8,256,256]{3,2,1,0:T(8,128)(2,1)} async-done(((bf16[2,1,256,256]{3,2,1,0:T(8,128)(2,1)}), bf16[2,8,256,256]{3,2,1,0:T(8,128)(2,1)}) %all-gather.2.cloned.1.call-update) | async-done | bytes 2097168 | tf_op jit(solution)/shard_map/all_gather | solution.py:38
  61.4 4.3 %gather_fusion = bf16[16,2,256,256]{3,2,1,0:T(8,128)(2,1)} fusion(bf16[2,8,256,256]{3,2,1,0:T(8,128)(2,1)} %all-gather.2.cloned.1.call-done, s32[1024]{0:T(1024)S(1)} %pad_clamp_fusion), kind=kCustom, calls=%fused_computation | custom fusion | bytes 8388672 | tf_op jit(solution)/shard_map/jit(_take)/gather | solution.py:39
  65.7 4.7 %fusion.2 = bf16[16,2,256,256]{3,2,1,0:T(8,128)(2,1)} fusion(bf16[16,2,256,256]{3,2,1,0:T(8,128)(2,1)} %gather_fusion, pred[16]{0:T(512)(128)(4,1)S(1)} %compare_and_fusion, bf16[1,16,256,256]{2,3,1,0:T(8,128)(2,1)S(1)} %copy.12, pred[16,256]{1,0:T(8,128)(4,1)S(1)} %iota_compare_fusion, pred[256]{0:T(512)(128)(4,1)S(1)} %iota_compare_fusion.2), kind=kOutput, calls=%fused_computation.3 | convolution fusion | flops 1077936128 | bytes 10490128 | tf_op jit(solution)/shard_map/bac,hbxc->bhax/dot_general | solution.py:40
  70.4 7.9 %copy.16 = bf16[16,2,256,256]{2,0,3,1:T(8,128)(2,1)} copy(bf16[16,2,256,256]{3,2,1,0:T(8,128)(2,1)} %fusion.2) | data formatting | bytes 8388608 | tf_op jit(solution)/shard_map/bac,hbxc->bhax/dot_general | solution.py:40
  78.3 0.0 copy-done.1
  78.3 3.4 %convert_bitcast_fusion = bf16[16,2,256,256]{3,0,2,1:T(8,128)(2,1)S(1)} fusion(bf16[16,2,256,256]{2,0,3,1:T(8,128)(2,1)} %copy.16, bf16[2,16,16]{2,1,0:T(8,128)(2,1)S(1)} %copy-done.1, pred[16,16]{1,0:T(8,128)(4,1)S(1)} %broadcast_compare_fusion), kind=kOutput, calls=%fused_computation.8 | convolution fusion | flops 69206528 | bytes 8389888 | tf_op jit(solution)/shard_map/nhst,nthac->nshac/dot_general | solution.py:46
  81.7 6.1 %fusion.11 = f32[1,16,256,256]{2,3,1,0:T(8,128)} fusion(bf16[16,2,256,256]{3,0,2,1:T(8,128)(2,1)S(1)} %convert_bitcast_fusion, bf16[2,1,256,256]{3,2,1,0:T(8,128)(2,1)S(1)} %copy-done), kind=kOutput, calls=%fused_computation.11 | convolution fusion | flops 1073741824 | bytes 8650752 | tf_op jit(solution)/shard_map/hnab,nshbc->nsac/dot_general | solution.py:49
  87.8 75.9 %all-reduce.1 = bf16[1,16,256,256]{2,3,1,0:T(8,128)(2,1)S(1)} all-reduce(f32[1,16,256,256]{2,3,1,0:T(8,128)} %fusion.11), channel_id=1, replica_groups=mesh['bond'=8,'mpo'=4] {'mpo'}, use_global_device_ids=true, to_apply=%region_2.3 | all-reduce | flops 1048576 | bytes 6291456 | tf_op jit(solution)/shard_map/psum | solution.py:54
  163.7 1.1 select_convert_fusion
  164.8 1.0 copy.14
  (9 shorter events, 0.0 us)
Async XLA Ops:
  6.5 75.1 %copy-start = (bf16[2,1,256,256]{3,2,1,0:T(8,128)(2,1)S(1)}, bf16[2,1,256,256]{3,2,1,0:T(8,128)(2,1)}, u32[]{:S(2)}) copy-start(bf16[2,1,256,256]{3,2,1,0:T(8,128)(2,1)} %param.9) | copy-start | bytes 786436
  6.5 3.6 %copy-start.5 = (s32[8]{0:T(128)S(1)}, s32[8]{0:T(128)}, u32[]{:S(2)}) copy-start(s32[8]{0:T(128)} %param.13) | copy-start | bytes 100
  6.5 4.9 %copy-start.2 = (s32[1,16,1]{1,2,0:T(1,128)S(1)}, s32[1,16,1]{1,2,0:T(1,128)}, u32[]{:S(2)}) copy-start(s32[1,16,1]{1,2,0:T(1,128)} %param.12) | copy-start | bytes 196
  6.5 4.9 %copy-start.3 = (s32[8]{0:T(128)S(1)}, s32[8]{0:T(128)}, u32[]{:S(2)}) copy-start(s32[8]{0:T(128)} %param.14) | copy-start | bytes 100
  6.5 4.9 %copy-start.4 = (s32[8]{0:T(128)S(1)}, s32[8]{0:T(128)}, u32[]{:S(2)}) copy-start(s32[8]{0:T(128)} %param.15) | copy-start | bytes 100
  6.5 54.8 %all-gather.2.cloned.1.call-start = ((), (), s32[]{:S(2)}) async-start(), calls=%async_computation | async-start | bytes 2359296 | tf_op jit(solution)/shard_map/all_gather | solution.py:38
  70.4 7.9 %copy-start.1 = (bf16[2,16,16]{2,1,0:T(8,128)(2,1)S(1)}, bf16[2,16,16]{2,1,0:T(8,128)(2,1)}, u32[]{:S(2)}) copy-start(bf16[2,16,16]{2,1,0:T(8,128)(2,1)} %param.11) | copy-start | bytes 3076
Sparse Core Ops, SparseCore 0:
  9.5 51.7 all-gather.1
where the time goes:
time: 173 us
  blocking collectives  75.9 us (44%)
  waiting for transfers between devices  48.3 us (28%)
  local copies, waits for them, and re-layouts  16.7 us (10%)
  matrix products  14.2 us (8%)
  between operations  13.5 us (8%)
  other arithmetic  4.04 us (2%)
    psum x1, blocking collectives, shards(): summed = lax.psum(partial_value, 'mpo')  75.9 us
    all_gather x1, waiting for transfers between devices, shards(): gathered = lax.all_gather(right_environment, 'bond', axis=1, tiled=True)  47.6 us
    dot_general x1, local copies, waits for them, and re-layouts, shards(): jnp.einsum('bac,hbxc->bhax', flat_blocks, chosen, preferred_element_type=...  7.89 us
    dot_general x1, matrix products, shards(): jnp.einsum('hnab,nshbc->nsac', left_environment, mixed, preferred_element...  6.13 us
    dot_general x1, matrix products, shards(): jnp.einsum('bac,hbxc->bhax', flat_blocks, chosen, preferred_element_type=...  4.66 us
    gather x1, local copies, waits for them, and re-layouts, shards(): chosen = jnp.take(gathered, place_flat, axis=1)  4.34 us
  transfers between devices with their start and end apart: 1, of which 1 were waited for; matrix products, arithmetic and copies ran while one was open for 4% of the time, Pallas kernels for 0%

commit v1 on v0

--- a/solution.py
+++ b/solution.py
@@ -35,7 +35,15 @@
     block_count = sectors * states
     flat_blocks = masked.reshape(block_count, block_rows, block_rows)
     place_flat = lookup(sector_place, sector_ids).reshape(block_count)
-    gathered = lax.all_gather(right_environment, "bond", axis=1, tiled=True)
+    ways, here, step = (lax.axis_size("bond"), lax.axis_index("bond"), right_environment.shape[1])
+    line, have = (right_environment, 1)
+    while have < ways:
+        line = jnp.concatenate(
+            [line, lax.ppermute(line, "bond", [(d, (d - have) % ways) for d in range(ways)])],
+            axis=1,
+        )
+        have = 2 * have
+    gathered = jnp.roll(line, here * step, axis=1)
     chosen = jnp.take(gathered, place_flat, axis=1)
     right_part = jnp.einsum(
         "bac,hbxc->bhax", flat_blocks, chosen, preferred_element_type=jnp.float32

time: 173 us -> 179 us (1.035)
  between operations: 13.5 us -> 0.13 us
  starting transfers between devices: 0.04 us -> 8.07 us
  waiting for transfers between devices: 48.3 us -> 55.1 us
  other arithmetic: 4.04 us -> 5.84 us
    ppermute x0 -> x3, waiting for transfers between devices: none -> 55.1 us  [shards(): lax.ppermute(line, 'bond', [(d, (d - have) % ways) for d in range(ways)])]
    all_gather x1 -> x0, waiting for transfers between devices: 47.6 us -> none  [shards(): gathered = lax.all_gather(right_environment, 'bond', axis=1, tiled=True)]
    ppermute x0 -> x3, starting transfers between devices: none -> 8.07 us  [shards(): lax.ppermute(line, 'bond', [(d, (d - have) % ways) for d in range(ways)])]
    unnamed x13 -> x18, local copies, waits for them, and re-layouts: 2.88 us -> 4.13 us
  transfers between devices with their start and end apart: 1 -> 3, of which waited for: 1 -> 3; matrix products, arithmetic and copies ran while one was open for 4% -> 5% of each run, Pallas kernels for 0% -> 0%
where the time goes in v1:
time: 179 us; the launch traced here: 178 us
  blocking collectives  76.1 us (43%)
  waiting for transfers between devices  55.1 us (31%)
  local copies, waits for them, and re-layouts  16.7 us (9%)
  matrix products  15.8 us (9%)
  starting transfers between devices  8.07 us (5%)
  other arithmetic  5.84 us (3%)
    psum x1, blocking collectives, shards(): summed = lax.psum(partial_value, 'mpo')  76.1 us
    ppermute x3, waiting for transfers between devices, shards(): lax.ppermute(line, 'bond', [(d, (d - have) % ways) for d in range(ways)])  55.1 us
    ppermute x3, starting transfers between devices, shards(): lax.ppermute(line, 'bond', [(d, (d - have) % ways) for d in range(ways)])  8.07 us
    dot_general x1, local copies, waits for them, and re-layouts, shards(): jnp.einsum('bac,hbxc->bhax', flat_blocks, chosen, preferred_element_type=...  7.94 us
    dot_general x1, matrix products, shards(): jnp.einsum('bac,hbxc->bhax', flat_blocks, chosen, preferred_element_type=...  6.23 us
    dot_general x1, matrix products, shards(): jnp.einsum('hnab,nshbc->nsac', left_environment, mixed, preferred_element...  6.13 us
    unnamed x18, local copies, waits for them, and re-layouts  4.13 us
  transfers between devices with their start and end apart: 3, of which 3 were waited for; matrix products, arithmetic and copies ran while one was open for 5% of the time, Pallas kernels for 0%

profile of v1, /device:TPU:0, one launch (start us, length us, event | category | flops | bytes accessed | tf_op | source)
XLA Modules:
  0.0 177.7 jit_solution(15616150840104633908)
XLA Ops:
  0.0 6.1 %collective-permute-start = (bf16[2,1,256,256]{3,2,1,0:T(8,128)(2,1)}, bf16[2,1,256,256]{3,2,1,0:T(8,128)(2,1)S(1)}, u32[]{:S(2)}, u32[]{:S(2)}) collective-permute-start(bf16[2,1,256,256]{3,2,1,0:T(8,128)(2,1)} %param.10), channel_id=1, source_target_pairs={{0,28},{4,0},{8,4},{12,8},{16,12},{20,16},{24,20},{28,24},{1,29},{... | collective-permute-start | bytes 786440 | tf_op jit(solution)/shard_map/ppermute | solution.py:42
  6.1 0.8 select_reduce_fusion.1
  6.9 5.1 %collective-permute-done = bf16[2,1,256,256]{3,2,1,0:T(8,128)(2,1)S(1)} collective-permute-done((bf16[2,1,256,256]{3,2,1,0:T(8,128)(2,1)}, bf16[2,1,256,256]{3,2,1,0:T(8,128)(2,1)S(1)}, u32[]{:S(2)}, u32[]{:S(2)}) %collective-permute-start) | collective-permute-done | bytes 262176 | tf_op jit(solution)/shard_map/ppermute | solution.py:42
  12.0 1.0 pad_maximum_fusion.1
  13.0 1.5 collective-permute-start.1
  14.5 3.9 %copy.12 = bf16[1,16,256,256]{2,3,1,0:T(8,128)(2,1)} copy(bf16[1,16,256,256]{3,2,1,0:T(8,128)(2,1)} %param.8) | data formatting | bytes 4194304 | tf_op args[0]
  18.4 0.6 dynamic_slice.13
  19.0 6.8 %collective-permute-done.1 = bf16[2,2,256,256]{3,2,1,0:T(8,128)(2,1)S(1)} collective-permute-done((bf16[2,2,256,256]{3,2,1,0:T(8,128)(2,1)S(1)}, bf16[2,2,256,256]{3,2,1,0:T(8,128)(2,1)S(1)}, u32[]{:S(2)}, u32[]{:S(2)}) %collective-permute-start.1) | collective-permute-done | bytes 524320 | tf_op jit(solution)/shard_map/ppermute | solution.py:42
  25.8 0.1 pad_maximum_fusion
  25.9 0.5 collective-permute-start.2
  26.4 0.6 iota_compare_fusion.2
  27.1 0.1 broadcast_compare_fusion
  27.2 0.1 iota_compare_fusion
  27.2 2.0 %broadcast_and_fusion = pred[1,16,256,256]{2,3,1,0:T(8,128)(4,1)} fusion(pred[16,256]{1,0:T(8,128)(4,1)S(1)} %iota_compare_fusion, pred[256]{0:T(512)(128)(4,1)S(1)} %iota_compare_fusion.2), kind=kLoop, calls=%fused_computation.15 | loop fusion | flops 1048576 | bytes 1052928 | tf_op jit(solution)/shard_map/and | solution.py:33
  29.4 43.2 %collective-permute-done.2 = bf16[2,4,256,256]{3,2,1,0:T(8,128)(2,1)S(1)} collective-permute-done((bf16[2,4,256,256]{3,2,1,0:T(8,128)(2,1)S(1)}, bf16[2,4,256,256]{3,2,1,0:T(8,128)(2,1)S(1)}, u32[]{:S(2)}, u32[]{:S(2)}) %collective-permute-start.2) | collective-permute-done | bytes 1048608 | tf_op jit(solution)/shard_map/ppermute | solution.py:42
  72.8 0.2 constant_dynamic-slice_fusion
  73.0 2.8 %gather_fusion = bf16[16,2,256,256]{3,2,1,0:T(8,128)(2,1)} fusion(bf16[2,8,256,256]{3,2,1,0:T(8,128)(2,1)S(1)} %constant_dynamic-slice_fusion, s32[1024]{0:T(1024)S(1)} %pad_clamp_fusion), kind=kCustom, calls=%fused_computation | custom fusion | bytes 8388672 | tf_op jit(solution)/shard_map/jit(_take)/gather | solution.py:47
  75.7 6.2 %fusion.2 = bf16[16,2,256,256]{3,2,1,0:T(8,128)(2,1)} fusion(bf16[16,2,256,256]{3,2,1,0:T(8,128)(2,1)} %gather_fusion, pred[16]{0:T(512)(128)(4,1)S(1)} %compare_and_fusion, bf16[1,16,256,256]{2,3,1,0:T(8,128)(2,1)} %copy.12, pred[16,256]{1,0:T(8,128)(4,1)S(1)} %iota_compare_fusion, pred[256]{0:T(512)(128)(4,1)S(1)} %iota_compare_fusion.2), kind=kOutput, calls=%fused_computation.3 | convolution fusion | flops 1077936128 | bytes 10490128 | tf_op jit(solution)/shard_map/bac,hbxc->bhax/dot_general | solution.py:48
  82.0 7.9 %copy.16 = bf16[16,2,256,256]{2,0,3,1:T(8,128)(2,1)} copy(bf16[16,2,256,256]{3,2,1,0:T(8,128)(2,1)} %fusion.2) | data formatting | bytes 8388608 | tf_op jit(solution)/shard_map/bac,hbxc->bhax/dot_general | solution.py:48
  89.9 3.4 %convert_bitcast_fusion = bf16[16,2,256,256]{3,0,2,1:T(8,128)(2,1)S(1)} fusion(bf16[16,2,256,256]{2,0,3,1:T(8,128)(2,1)} %copy.16, bf16[2,16,16]{2,1,0:T(8,128)(2,1)S(1)} %copy-done.2, pred[16,16]{1,0:T(8,128)(4,1)S(1)} %broadcast_compare_fusion), kind=kOutput, calls=%fused_computation.8 | convolution fusion | flops 69206528 | bytes 8389888 | tf_op jit(solution)/shard_map/nhst,nthac->nshac/dot_general | solution.py:54
  93.4 6.1 %fusion.11 = f32[1,16,256,256]{2,3,1,0:T(8,128)} fusion(bf16[16,2,256,256]{3,0,2,1:T(8,128)(2,1)S(1)} %convert_bitcast_fusion, bf16[2,1,256,256]{3,2,1,0:T(8,128)(2,1)S(1)} %copy-done), kind=kOutput, calls=%fused_computation.11 | convolution fusion | flops 1073741824 | bytes 8650752 | tf_op jit(solution)/shard_map/hnab,nshbc->nsac/dot_general | solution.py:57
  99.5 76.1 %all-reduce.1 = bf16[1,16,256,256]{2,3,1,0:T(8,128)(2,1)S(1)} all-reduce(f32[1,16,256,256]{2,3,1,0:T(8,128)} %fusion.11), channel_id=1, replica_groups=mesh['bond'=8,'mpo'=4] {'mpo'}, use_global_device_ids=true, to_apply=%region_2.3 | all-reduce | flops 1048576 | bytes 6291456 | tf_op jit(solution)/shard_map/psum | solution.py:62
  175.6 1.1 select_convert_fusion
  176.7 1.0 copy.14
  (21 shorter events, 0.3 us)
Async XLA Ops:
  0.0 93.3 %copy-start = (bf16[2,1,256,256]{3,2,1,0:T(8,128)(2,1)S(1)}, bf16[2,1,256,256]{3,2,1,0:T(8,128)(2,1)}, u32[]{:S(2)}) copy-start(bf16[2,1,256,256]{3,2,1,0:T(8,128)(2,1)} %param.9) | copy-start | bytes 786436
  0.0 19.0 %copy-start.1 = (bf16[2,1,256,256]{3,2,1,0:T(8,128)(2,1)S(1)}, bf16[2,1,256,256]{3,2,1,0:T(8,128)(2,1)}, u32[]{:S(2)}) copy-start(bf16[2,1,256,256]{3,2,1,0:T(8,128)(2,1)} %param.10) | copy-start | bytes 786436
  0.0 27.1 %copy-start.3 = (s32[1,16,1]{1,2,0:T(1,128)S(1)}, s32[1,16,1]{1,2,0:T(1,128)}, u32[]{:S(2)}) copy-start(s32[1,16,1]{1,2,0:T(1,128)} %param.12) | copy-start | bytes 196
  0.0 18.4 %copy-start.4 = (s32[8]{0:T(128)S(1)}, s32[8]{0:T(128)}, u32[]{:S(2)}) copy-start(s32[8]{0:T(128)} %param.13) | copy-start | bytes 100
  0.0 11.9 %collective-permute-start = (bf16[2,1,256,256]{3,2,1,0:T(8,128)(2,1)}, bf16[2,1,256,256]{3,2,1,0:T(8,128)(2,1)S(1)}, u32[]{:S(2)}, u32[]{:S(2)}) collective-permute-start(bf16[2,1,256,256]{3,2,1,0:T(8,128)(2,1)} %param.10), channel_id=1, source_target_pairs={{0,28},{4,0},{8,4},{12,8},{16,12},{20,16},{24,20},{28,24},{1,29},{... | collective-permute-start | bytes 786440 | tf_op jit(solution)/shard_map/ppermute | solution.py:42
  13.0 12.9 %collective-permute-start.1 = (bf16[2,2,256,256]{3,2,1,0:T(8,128)(2,1)S(1)}, bf16[2,2,256,256]{3,2,1,0:T(8,128)(2,1)S(1)}, u32[]{:S(2)}, u32[]{:S(2)}) collective-permute-start(bf16[2,2,256,256]{3,2,1,0:T(8,128)(2,1)S(1)} %pad_maximum_fusion.1), channel_id=1, source_target_pairs={{0,24},{4,28},{8,0},{12,4},{16,8},{20,12},{24,16},{28,20},{1,25},{... | collective-permute-start | bytes 1572872 | tf_op jit(solution)/shard_map/ppermute | solution.py:42
  25.9 46.6 %collective-permute-start.2 = (bf16[2,4,256,256]{3,2,1,0:T(8,128)(2,1)S(1)}, bf16[2,4,256,256]{3,2,1,0:T(8,128)(2,1)S(1)}, u32[]{:S(2)}, u32[]{:S(2)}) collective-permute-start(bf16[2,4,256,256]{3,2,1,0:T(8,128)(2,1)S(1)} %pad_maximum_fusion), channel_id=1, source_target_pairs={{0,16},{4,20},{8,24},{12,28},{16,0},{20,4},{24,8},{28,12},{1,17},{... | collective-permute-start | bytes 3145736 | tf_op jit(solution)/shard_map/ppermute | solution.py:42
  82.0 7.9 %copy-start.2 = (bf16[2,16,16]{2,1,0:T(8,128)(2,1)S(1)}, bf16[2,16,16]{2,1,0:T(8,128)(2,1)}, u32[]{:S(2)}) copy-start(bf16[2,16,16]{2,1,0:T(8,128)(2,1)} %param.11) | copy-start | bytes 3076
